TPU v7x, 32 devices: a whole 2x2x4 slice. The times are simulated.
32 devices in a mesh: dp: 8 (over z, y), mix: 4 (over x, core).
Axes of the slice: x: 2, y: 2, z: 4, core: 2. Of those that a mesh axis runs over, the one named last changes fastest.
Arguments:
- patches: bfloat16 [224, 196, 768], P('dp', 'mix'), may hold values from -6 to 6
- valid_counts: int32 [8], P('dp'), may hold values from 7 to 28, as said below
- gain_one: float32 [768], replicated, may hold values from 0.5 to 1.5
- shift_one: float32 [768], replicated, may hold values from -1.25 to 1.25
- tok_in: bfloat16 [196, 384], replicated, may hold values from -0.4375 to 0.4375
- tok_inbias: float32 [384], replicated, may hold values from -1.25 to 1.25
- tok_out: bfloat16 [384, 196], replicated, may hold values from -0.3125 to 0.3125
- tok_outbias: float32 [196], replicated, may hold values from -1.25 to 1.25
- gain_two: float32 [768], replicated, may hold values from 0.5 to 1.5
- shift_two: float32 [768], replicated, may hold values from -1.25 to 1.25
- chan_in: bfloat16 [768, 3072], replicated, may hold values from -0.21875 to 0.21875
- chan_inbias: float32 [3072], replicated, may hold values from -1.25 to 1.25
- chan_out: bfloat16 [3072, 768], replicated, may hold values from -0.109375 to 0.109375
- chan_outbias: float32 [768], replicated, may hold values from -1.25 to 1.25
- out_grad: bfloat16 [224, 196, 768], P('dp', 'mix'), may hold values from -6 to 6
Outputs:
- mixed_out: bfloat16 [224, 196, 768], P('dp', 'mix')
- patch_grad: bfloat16 [224, 196, 768], P('dp', 'mix')
- grad_gain_one: float32 [768], replicated
- grad_shift_one: float32 [768], replicated
- grad_tok_in: float32 [196, 384], replicated
- grad_tok_inbias: float32 [384], replicated
- grad_tok_out: float32 [384, 196], replicated
- grad_tok_outbias: float32 [196], replicated
- grad_gain_two: float32 [768], replicated
- grad_shift_two: float32 [768], replicated
- grad_chan_in: float32 [768, 3072], replicated
- grad_chan_inbias: float32 [3072], replicated
- grad_chan_out: float32 [3072, 768], replicated
- grad_chan_outbias: float32 [768], replicated
Inputs may be any that keep to these rules, and one draw needn't show every extreme that they name: `valid_counts`: how many of the 28 images of each index of dp are real; the rest are padding and get no gradient.
All inputs are finite; a program needn't handle non-finite values.
Results may differ from a plain program's by a relative error of at most 0.008.
Values may be sent and summed in bfloat16 or wider, within the bound.
A program may use at most 192 MiB of HBM per device.

v0:
```python
import jax
import jax.numpy as jnp
from jax import lax
from jax.sharding import PartitionSpec as P

EPS = 1e-06


def layer_norm(values, gain, shift):
    center = values - jnp.mean(values, axis=-1, keepdims=True)
    spread = jnp.mean(center * center, axis=-1, keepdims=True)
    return center * lax.rsqrt(spread + EPS) * gain + shift


def shards(
    patches,
    valid_counts,
    gain_one,
    shift_one,
    tok_in,
    tok_inbias,
    tok_out,
    tok_outbias,
    gain_two,
    shift_two,
    chan_in,
    chan_inbias,
    chan_out,
    chan_outbias,
    out_grad,
):
    images, part, width = patches.shape
    rowcount = images * part
    inputs = patches.astype(jnp.float32)
    normed_full, first_back = jax.vjp(layer_norm, inputs, gain_one, shift_one)
    normed = normed_full.astype(jnp.bfloat16)
    columns = lax.all_to_all(normed, "mix", split_axis=2, concat_axis=1, tiled=True)
    widened = (
        jnp.einsum("bsc,sk->bkc", columns, tok_in, preferred_element_type=jnp.float32)
        + tok_inbias[None, :, None]
    )
    hidden = jax.nn.gelu(widened).astype(jnp.bfloat16)
    mixed_cols = (
        jnp.einsum("bkc,ks->bsc", hidden, tok_out, preferred_element_type=jnp.float32)
        + tok_outbias[None, :, None]
    ).astype(jnp.bfloat16)
    mixed = lax.all_to_all(mixed_cols, "mix", split_axis=1, concat_axis=2, tiled=True)
    middle = inputs + mixed.astype(jnp.float32)
    second_full, second_back = jax.vjp(layer_norm, middle, gain_two, shift_two)
    second = second_full.astype(jnp.bfloat16).reshape(rowcount, width)
    inner = jnp.dot(second, chan_in, preferred_element_type=jnp.float32) + chan_inbias
    activ = jax.nn.gelu(inner).astype(jnp.bfloat16)
    branch = jnp.dot(activ, chan_out, preferred_element_type=jnp.float32) + chan_outbias
    mixed_out = (middle + branch.reshape(images, part, width)).astype(jnp.bfloat16)
    live = jnp.arange(images, dtype=jnp.int32) < valid_counts[0]
    upstream = jnp.where(live[:, None, None], out_grad, jnp.zeros_like(out_grad)).reshape(
        rowcount, width
    )
    inner_again = jnp.dot(second, chan_in, preferred_element_type=jnp.float32) + chan_inbias
    activ_full, chan_gelu_back = jax.vjp(jax.nn.gelu, inner_again)
    activ_again = activ_full.astype(jnp.bfloat16)
    grad_chan_out = jnp.einsum(
        "rf,rc->fc", activ_again, upstream, preferred_element_type=jnp.float32
    )
    grad_chan_outbias = jnp.sum(upstream.astype(jnp.float32), axis=0)
    grad_activ = jnp.einsum("rc,fc->rf", upstream, chan_out, preferred_element_type=jnp.float32)
    grad_inner = chan_gelu_back(grad_activ)[0].astype(jnp.bfloat16)
    grad_chan_in = jnp.einsum("rc,rf->cf", second, grad_inner, preferred_element_type=jnp.float32)
    grad_chan_inbias = jnp.sum(grad_inner.astype(jnp.float32), axis=0)
    grad_second = jnp.einsum("rf,cf->rc", grad_inner, chan_in, preferred_element_type=jnp.float32)
    grad_middle, grad_gain_two, grad_shift_two = second_back(
        grad_second.reshape(images, part, width)
    )
    grad_middle = grad_middle + upstream.astype(jnp.float32).reshape(images, part, width)
    grad_cols = lax.all_to_all(
        grad_middle.astype(jnp.bfloat16), "mix", split_axis=2, concat_axis=1, tiled=True
    )
    widened_again = (
        jnp.einsum("bsc,sk->bkc", columns, tok_in, preferred_element_type=jnp.float32)
        + tok_inbias[None, :, None]
    )
    hidden_full, tok_gelu_back = jax.vjp(jax.nn.gelu, widened_again)
    hidden_again = hidden_full.astype(jnp.bfloat16)
    grad_tok_out = jnp.einsum(
        "bkc,bsc->ks", hidden_again, grad_cols, preferred_element_type=jnp.float32
    )
    grad_tok_outbias = jnp.sum(grad_cols.astype(jnp.float32), axis=(0, 2))
    grad_hidden = jnp.einsum("ks,bsc->bkc", tok_out, grad_cols, preferred_element_type=jnp.float32)
    grad_widened = tok_gelu_back(grad_hidden)[0].astype(jnp.bfloat16)
    grad_tok_in = jnp.einsum(
        "bsc,bkc->sk", columns, grad_widened, preferred_element_type=jnp.float32
    )
    grad_tok_inbias = jnp.sum(grad_widened.astype(jnp.float32), axis=(0, 2))
    grad_columns = jnp.einsum(
        "sk,bkc->bsc", tok_in, grad_widened, preferred_element_type=jnp.float32
    ).astype(jnp.bfloat16)
    grad_normed = lax.all_to_all(grad_columns, "mix", split_axis=1, concat_axis=2, tiled=True)
    grad_inputs, grad_gain_one, grad_shift_one = first_back(grad_normed.astype(jnp.float32))
    patch_grad = (grad_middle + grad_inputs).astype(jnp.bfloat16)
    summed = lax.psum(
        (
            grad_gain_one,
            grad_shift_one,
            grad_tok_in,
            grad_tok_inbias,
            grad_tok_out,
            grad_tok_outbias,
            grad_gain_two,
            grad_shift_two,
            grad_chan_in,
            grad_chan_inbias,
            grad_chan_out,
            grad_chan_outbias,
        ),
        ("dp", "mix"),
    )
    return (
        mixed_out,
        patch_grad,
        summed[0],
        summed[1],
        summed[2],
        summed[3],
        summed[4],
        summed[5],
        summed[6],
        summed[7],
        summed[8],
        summed[9],
        summed[10],
        summed[11],
    )


def solution(mesh):
    return jax.shard_map(
        shards,
        mesh=mesh,
        in_specs=(
            P("dp", "mix", None),
            P("dp"),
            P(),
            P(),
            P(),
            P(),
            P(),
            P(),
            P(),
            P(),
            P(),
            P(),
            P(),
            P(),
            P("dp", "mix", None),
        ),
        out_specs=(
            P("dp", "mix", None),
            P("dp", "mix", None),
            P(),
            P(),
            P(),
            P(),
            P(),
            P(),
            P(),
            P(),
            P(),
            P(),
            P(),
            P(),
        ),
        check_vma=False,
    )
```

profile of v0, /device:TPU:0, one launch (start us, length us, event | category | flops | bytes accessed | tf_op | source)
XLA Modules:
  0.0 723.8 jit_solution(6114710992727440725)
XLA Ops:
  15.3 11.4 %copy.67 = bf16[28,49,768]{1,0,2:T(8,128)(2,1)} copy(bf16[28,49,768]{2,1,0:T(8,128)(2,1)} %fusion.25) | data formatting | bytes 4214784 | tf_op jit(solution)/shard_map/convert_element_type | solution.py:36
  26.7 11.5 %reshape.138 = bf16[4,2,131712]{2,1,0:T(2,128)(2,1)} reshape(bf16[768,28,49]{2,1,0:T(8,128)(2,1)} %bitcast.86) | data formatting | bytes 4214784
  38.2 31.3 %all_to_all.54 = bf16[4,2,131712]{2,1,0:T(2,128)(2,1)} all-to-all(bf16[4,2,131712]{2,1,0:T(2,128)(2,1)} %reshape.138), channel_id=1, replica_groups=mesh['dp'=8,'mix'=4] {'mix'}, dimensions={0} | all-to-all | bytes 4214784 | tf_op jit(solution)/shard_map/all_to_all | solution.py:37
  69.6 11.9 %reshape.139 = bf16[768,28,49]{2,1,0:T(8,128)(2,1)} reshape(bf16[4,2,131712]{2,1,0:T(2,128)(2,1)} %all_to_all.54) | data formatting | bytes 4214784
  81.5 9.6 %copy.68 = bf16[28,49,4,192]{3,1,2,0:T(8,128)(2,1)} copy(bf16[28,49,4,192]{1,0,3,2:T(8,128)(2,1)} %bitcast.84) | data formatting | bytes 4214784 | tf_op jit(solution)/shard_map/all_to_all | solution.py:37
  96.8 7.8 %fusion.17 = (bf16[28,384,192]{1,2,0:T(8,128)(2,1)S(1)}, f32[28,192,384]{2,1,0:T(8,128)}) fusion(f32[384]{0:T(512)S(1)} %copy-done.29, bf16[28,196,192]{2,1,0:T(8,128)(2,1)} %all_to_all.43, bf16[196,384]{1,0:T(8,128)(2,1)S(1)} %copy-done), kind=kOutput, calls=%fused_computation.26 | convolution fusion | flops 829882368 | bytes 14645760 | tf_op jit(solution)/shard_map/bsc,sk->bkc/dot_general | solution.py:39
  109.7 7.4 %copy.70 = bf16[28,196,192]{2,0,1:T(8,128)(2,1)} copy(bf16[28,196,192]{1,2,0:T(8,128)(2,1)} %fusion.30) | data formatting | bytes 4214784 | tf_op jit(solution)/shard_map/convert_element_type | solution.py:46
  131.1 28.5 %all-to-all-done.1 = bf16[28,196,192]{2,0,1:T(8,128)(2,1)} async-done(((bf16[28,196,192]{2,0,1:T(8,128)(2,1)}), bf16[28,196,192]{2,0,1:T(8,128)(2,1)}, u32[]{:S(2)}, u32[]{:S(2)}) %all-to-all-start.1) | async-done | bytes 2107424 | tf_op jit(solution)/shard_map/all_to_all | solution.py:47
  159.6 7.5 %copy.71 = bf16[28,196,192]{1,2,0:T(8,128)(2,1)} copy(bf16[28,196,192]{2,0,1:T(8,128)(2,1)} %all-to-all-done.1) | data formatting | bytes 4214784 | tf_op jit(solution)/shard_map/all_to_all | solution.py:47
  179.2 7.5 %copy.73 = f32[28,49,4,192]{3,2,1,0:T(4,128)} copy(f32[28,49,4,192]{3,1,2,0:T(8,128)} %bitcast.82) | data formatting | bytes 8429568 | tf_op jit(solution)/shard_map/convert_element_type | solution.py:48
  186.6 7.7 %reshape.130 = f32[28,49,768]{2,1,0:T(8,128)} reshape(f32[28,49,4,192]{3,2,1,0:T(4,128)} %copy.73) | data formatting | bytes 8429568 | tf_op jit(solution)/shard_map/convert_element_type | solution.py:48
  202.4 17.7 %multiply_convert_fusion = (bf16[1372,3072]{1,0:T(8,128)(2,1)}, f32[1372,3072]{1,0:T(8,128)}) fusion(f32[3072]{0:T(1024)S(1)} %copy-done.27, bf16[1372,768]{1,0:T(8,128)(2,1)} %reshape.126, bf16[768,3072]{1,0:T(8,128)(2,1)} %param.25), kind=kOutput, calls=%fused_computation.10 | convolution fusion | flops 6516056064 | bytes 32126976 | tf_op jit(solution)/shard_map/dot_general | solution.py:51
  220.2 19.9 %convert_reduce_fusion = (f32[3072]{0:T(1024)S(1)}, bf16[1372,3072]{1,0:T(8,128)(2,1)S(1)}) fusion(f32[1372,3072]{1,0:T(8,128)} %get-tuple-element.40, f32[3072]{0:T(1024)S(1)} %copy-done.27, bf16[1372,768]{1,0:T(8,128)(2,1)S(1)} %copy-done.11, bf16[3072,768]{1,0:T(8,128)(2,1)} %param.27), kind=kOutput, calls=%fused_computation.9 | convolution fusion | flops 6570845184 | bytes 32139264 | tf_op jit(solution)/shard_map/rc,fc->rf/dot_general | solution.py:66
  240.1 8.3 %fusion.41 = (f32[768]{0:T(1024)S(1)}, f32[1372,768]{1,0:T(8,128)}) fusion(bf16[1372,3072]{1,0:T(8,128)(2,1)S(1)} %get-tuple-element.46, bf16[768,3072]{1,0:T(8,128)(2,1)S(1)} %bitcast.92), kind=kOutput, calls=%fused_computation.81 | convolution fusion | flops 6474960896 | bytes 17366016 | tf_op jit(solution)/shard_map/rf,cf->rc/dot_general | solution.py:70
  258.3 12.2 %convolution_add_fusion = f32[1372,768]{1,0:T(8,128)} fusion(bf16[1372,3072]{1,0:T(8,128)(2,1)} %get-tuple-element.39, bf16[3072,768]{1,0:T(8,128)(2,1)} %param.27, f32[768]{0:T(1024)S(1)} %copy-done.28), kind=kOutput, calls=%fused_computation.54 | convolution fusion | flops 6474961920 | bytes 17366016 | tf_op jit(solution)/shard_map/dot_general | solution.py:53
  275.8 7.4 %fusion.39 = (f32[28,49]{1,0:T(8,128)S(1)}, f32[28,49,768]{2,1,0:T(8,128)S(1)}, bf16[28,49,768]{2,1,0:T(8,128)(2,1)}) fusion(f32[28,49]{1,0:T(8,128)S(1)} %multiply_multiply_fusion.5, f32[28,49,768]{2,1,0:T(8,128)} %copy-done.1, f32[28,49]{1,0:T(8,128)S(1)} %broadcast_multiply_fusion, f32[28,49]{1,0:T(8,128)S(1)} %fusion.38, f32[28,49,768]{2,1,0:T(8,128)} %reshape.129, ...), kind=kLoop, calls=%fused_computation.79 | loop fusion | flops 9481892 | bytes 18991552 | tf_op jit(solution)/shard_map/transpose(jvp())/reduce_sum | solution.py:10
  285.9 10.8 %copy.74 = bf16[28,49,768]{1,0,2:T(8,128)(2,1)} copy(bf16[28,49,768]{2,1,0:T(8,128)(2,1)S(1)} %fusion.29) | data formatting | bytes 4214784 | tf_op jit(solution)/shard_map/convert_element_type | solution.py:76
  296.8 11.5 %reshape.140 = bf16[4,2,131712]{2,1,0:T(2,128)(2,1)} reshape(bf16[768,28,49]{2,1,0:T(8,128)(2,1)} %bitcast.87) | data formatting | bytes 4214784
  312.0 13.2 %fusion.43 = f32[3072,768]{1,0:T(8,128)} fusion(bf16[1372,3072]{1,0:T(8,128)(2,1)} %get-tuple-element.39, bf16[1372,768]{1,0:T(8,128)(2,1)} %reshape.128), kind=kOutput, calls=%fused_computation.83 | convolution fusion | flops 6473908224 | bytes 19974144 | tf_op jit(solution)/shard_map/rf,rc->fc/dot_general | solution.py:62
  325.1 12.2 %fusion.42 = f32[768,3072]{1,0:T(8,128)} fusion(bf16[1372,768]{1,0:T(8,128)(2,1)S(1)} %copy-done.12, bf16[1372,3072]{1,0:T(8,128)(2,1)} %copy-done.33), kind=kOutput, calls=%fused_computation.82 | convolution fusion | flops 6473908224 | bytes 19974144 | tf_op jit(solution)/shard_map/rc,rf->cf/dot_general | solution.py:68
  337.7 10.9 %reshape.141 = bf16[768,28,49]{2,1,0:T(8,128)(2,1)} reshape(bf16[4,2,131712]{2,1,0:T(2,128)(2,1)S(1)} %all-to-all-done.2) | data formatting | bytes 4214784
  348.6 8.6 %copy.75 = bf16[28,49,4,192]{3,1,2,0:T(8,128)(2,1)S(1)} copy(bf16[28,49,4,192]{1,0,3,2:T(8,128)(2,1)} %bitcast.85) | data formatting | bytes 4214784 | tf_op jit(solution)/shard_map/all_to_all | solution.py:75
  365.4 9.6 %convert_reduce_fusion.1 = (f32[384]{0:T(512)S(1)}, bf16[28,384,192]{1,2,0:T(8,128)(2,1)S(1)}) fusion(f32[28,192,384]{2,1,0:T(8,128)} %get-tuple-element.38, f32[384]{0:T(512)S(1)} %copy-done.30, bf16[28,196,192]{2,1,0:T(8,128)(2,1)S(1)} %copy-done.10, bf16[384,196]{0,1:T(8,128)(2,1)S(1)} %copy-done.26), kind=kOutput, calls=%fused_computation.27 | convolution fusion | flops 856718976 | bytes 14647296 | tf_op jit(solution)/shard_map/ks,bsc->bkc/dot_general | solution.py:88
  384.6 7.5 %copy.77 = bf16[28,196,192]{2,0,1:T(8,128)(2,1)} copy(bf16[28,196,192]{1,2,0:T(8,128)(2,1)} %convert_bitcast_fusion) | data formatting | bytes 4214784 | tf_op jit(solution)/shard_map/convert_element_type | solution.py:96
  397.5 55.4 %all-to-all-done.3 = bf16[28,196,192]{2,0,1:T(8,128)(2,1)} async-done(((bf16[28,196,192]{2,0,1:T(8,128)(2,1)}), bf16[28,196,192]{2,0,1:T(8,128)(2,1)}, u32[]{:S(2)}, u32[]{:S(2)}) %all-to-all-start.3) | async-done | bytes 2107424 | tf_op jit(solution)/shard_map/all_to_all | solution.py:97
  452.9 7.0 copy.78
  463.7 7.0 reshape.133
  470.7 7.5 %copy.80 = f32[28,49,4,192]{3,2,1,0:T(4,128)} copy(f32[28,49,4,192]{3,1,2,0:T(8,128)} %bitcast.83) | data formatting | bytes 8429568 | tf_op jit(solution)/shard_map/convert_element_type | solution.py:98
  478.2 8.0 %reshape.131 = f32[28,49,768]{2,1,0:T(8,128)} reshape(f32[28,49,4,192]{3,2,1,0:T(4,128)} %copy.80) | data formatting | bytes 8429568 | tf_op jit(solution)/shard_map/convert_element_type | solution.py:98
  496.2 42.5 %all-reduce = (f32[768]{0:T(1024)}, f32[768]{0:T(1024)}, f32[384]{0:T(512)}, f32[196]{0:T(256)}, f32[768]{0:T(1024)}, /*index=5*/f32[768]{0:T(1024)}, f32[3072]{0:T(1024)}, f32[768]{0:T(1024)}) all-reduce(f32[768]{0:T(1024)S(1)} %get-tuple-element.16, f32[768]{0:T(1024)S(1)} %reduce_sum.199, ...), channel_id=1, replica_groups=mesh['dp'=8,'mix'=4] {'dp','mix'}, use_global_device_ids=true, to_apply=%region_9.10 | all-reduce | flops 7492 | bytes 59936 | tf_op jit(solution)/shard_map/psum | solution.py:100
  545.4 155.2 %all-reduce.4.cloned.1.call-done = (f32[196,384]{1,0:T(8,128)}, f32[384,196]{0,1:T(8,128)}, f32[768,3072]{1,0:T(8,128)}, f32[3072,768]{1,0:T(8,128)}) async-done(((f32[196,384]{1,0:T(8,128)}, f32[384,196]{0,1:T(8,128)}, f32[768,3072]{1,0:T(8,128)}, f32[3072,768]{1,0:T(8,128)}), (f32[196,384]{1,0:T(8,128)}, f32[384,196]{0,1:T(8,128)}, f32[768,3072]{1,0:T(8,128)}, ...) | async-done | bytes 19476496 | tf_op jit(solution)/shard_map/psum | solution.py:100
  704.2 8.8 %copy.95 = f32[768,3072]{1,0:T(8,128)} copy(f32[768,3072]{1,0:T(8,128)} %get-tuple-element.57) | data formatting | bytes 18874368
  (130 shorter events, 125.1 us)
Async XLA Ops:
  7.2 89.6 %copy-start = (bf16[196,384]{1,0:T(8,128)(2,1)S(1)}, bf16[196,384]{1,0:T(8,128)(2,1)}, u32[]{:S(2)}) copy-start(bf16[196,384]{1,0:T(8,128)(2,1)} %param.19) | copy-start | bytes 451588
  7.2 6.0 copy-start.2
  7.2 6.0 copy-start.19
  7.2 6.0 copy-start.23
  91.1 5.7 copy-start.29
  96.8 9.8 %copy-start.25 = (bf16[384,196]{0,1:T(8,128)(2,1)S(1)}, bf16[384,196]{0,1:T(8,128)(2,1)}, u32[]{:S(2)}) copy-start(bf16[384,196]{0,1:T(8,128)(2,1)} %param.21) | copy-start | bytes 451588
  96.8 9.8 %copy-start.31 = (f32[196]{0:T(256)S(1)}, f32[196]{0:T(256)}, u32[]{:S(2)}) copy-start(f32[196]{0:T(256)} %param.22) | copy-start | bytes 2356
  117.1 42.5 %all-to-all-start.1 = ((bf16[28,196,192]{2,0,1:T(8,128)(2,1)}), bf16[28,196,192]{2,0,1:T(8,128)(2,1)}, u32[]{:S(2)}, u32[]{:S(2)}) async-start(bf16[28,196,192]{2,0,1:T(8,128)(2,1)} %copy.70), calls=%async_computation.1 | async-start | bytes 6422528 | tf_op jit(solution)/shard_map/all_to_all | solution.py:47
  202.4 17.7 %copy-start.11 = (bf16[1372,768]{1,0:T(8,128)(2,1)S(1)}, bf16[1372,768]{1,0:T(8,128)(2,1)}, u32[]{:S(2)}) copy-start(bf16[1372,768]{1,0:T(8,128)(2,1)} %reshape.128) | copy-start | bytes 6322180
  202.4 37.7 %slice-start.3 = ((s8[4718592]{0:T(1024)(128)(4,1)}), s8[4194304]{0:T(1024)(128)(4,1)S(1)}, s32[]{:S(2)}) async-start(s8[4718592]{0:T(1024)(128)(4,1)} %bitcast.91), calls=%async_computation.8 | async-start | bytes 8388608
  220.2 20.0 %slice-start.4 = ((s8[4718592]{0:T(1024)(128)(4,1)}), s8[524288]{0:T(1024)(128)(4,1)S(1)}, s32[]{:S(2)}) async-start(s8[4718592]{0:T(1024)(128)(4,1)} %bitcast.91), calls=%async_computation.9 | async-start | bytes 1048576
  240.1 8.4 %copy-start.33 = (bf16[1372,3072]{1,0:T(8,128)(2,1)}, bf16[1372,3072]{1,0:T(8,128)(2,1)S(1)}, u32[]{:S(2)}) copy-start(bf16[1372,3072]{1,0:T(8,128)(2,1)S(1)} %get-tuple-element.46) | copy-start | bytes 25288708
  253.6 4.7 copy-start.28
  275.8 9.6 %copy-start.6 = (bf16[28,49,768]{2,1,0:T(8,128)(2,1)S(1)}, bf16[28,49,768]{2,1,0:T(8,128)(2,1)}, u32[]{:S(2)}) copy-start(bf16[28,49,768]{2,1,0:T(8,128)(2,1)} %get-tuple-element.31) | copy-start | bytes 6322180
  308.3 29.4 %all-to-all-start.2 = ((bf16[4,2,131712]{2,1,0:T(2,128)(2,1)}), bf16[4,2,131712]{2,1,0:T(2,128)(2,1)S(1)}, u32[]{:S(2)}, u32[]{:S(2)}) async-start(bf16[4,2,131712]{2,1,0:T(2,128)(2,1)} %reshape.140), calls=%async_computation.2 | async-start | bytes 4214784 | tf_op jit(solution)/shard_map/all_to_all | solution.py:75
  311.9 388.7 %all-reduce.4.cloned.1.call-start = ((), (), s32[]{:S(2)}) async-start(), calls=%async_computation.4 | async-start | bytes 38977536 | tf_op jit(solution)/shard_map/psum | solution.py:100
  311.9 13.2 %copy-start.12 = (bf16[1372,768]{1,0:T(8,128)(2,1)S(1)}, bf16[1372,768]{1,0:T(8,128)(2,1)}, u32[]{:S(2)}) copy-start(bf16[1372,768]{1,0:T(8,128)(2,1)} %reshape.126) | copy-start | bytes 6322180
  360.1 5.2 copy-start.10
  360.1 5.2 copy-start.26
  360.1 5.2 copy-start.30
  365.4 11.7 %copy-start.9 = (bf16[28,196,192]{2,1,0:T(8,128)(2,1)S(1)}, bf16[28,196,192]{2,1,0:T(8,128)(2,1)}, u32[]{:S(2)}) copy-start(bf16[28,196,192]{2,1,0:T(8,128)(2,1)} %all_to_all.43) | copy-start | bytes 6322180
  392.1 60.8 %all-to-all-start.3 = ((bf16[28,196,192]{2,0,1:T(8,128)(2,1)}), bf16[28,196,192]{2,0,1:T(8,128)(2,1)}, u32[]{:S(2)}, u32[]{:S(2)}) async-start(bf16[28,196,192]{2,0,1:T(8,128)(2,1)} %copy.77), calls=%async_computation.3 | async-start | bytes 6422528 | tf_op jit(solution)/shard_map/all_to_all | solution.py:97
  459.9 10.8 %copy-start.7 = (bf16[28,196,192]{1,2,0:T(8,128)(2,1)}, bf16[28,196,192]{1,2,0:T(8,128)(2,1)S(1)}, u32[]{:S(2)}) copy-start(bf16[28,196,192]{1,2,0:T(8,128)(2,1)S(1)} %copy.78) | copy-start | bytes 6322180
  478.2 10.5 %copy-start.3 = (bf16[28,49,768]{2,1,0:T(8,128)(2,1)S(1)}, bf16[28,49,768]{2,1,0:T(8,128)(2,1)}, u32[]{:S(2)}) copy-start(bf16[28,49,768]{2,1,0:T(8,128)(2,1)} %param.15) | copy-start | bytes 6322180
  478.2 10.5 %copy-start.14 = (f32[28,49]{1,0:T(8,128)S(1)}, f32[28,49]{1,0:T(8,128)}, u32[]{:S(2)}) copy-start(f32[28,49]{1,0:T(8,128)} %copy-done.13) | copy-start | bytes 16468
  478.2 10.5 %copy-start.20 = (f32[768]{0:T(1024)S(1)}, f32[768]{0:T(1024)}, u32[]{:S(2)}) copy-start(f32[768]{0:T(1024)} %param.17) | copy-start | bytes 9220
  488.5 4.0 copy-start.18
  488.5 4.1 copy-start.16
  488.8 4.9 copy-start.4
  702.3 10.6 %slice-start = ((s8[9437184]{0:T(1024)(128)(4,1)}), s8[4194304]{0:T(1024)(128)(4,1)S(1)}, s32[]{:S(2)}) async-start(s8[9437184]{0:T(1024)(128)(4,1)} %bitcast.89), calls=%async_computation.5 | async-start | bytes 8388608
  704.2 8.8 %slice-start.1 = ((s8[9437184]{0:T(1024)(128)(4,1)}), s8[4194304]{0:T(1024)(128)(4,1)S(1)}, s32[]{:S(2)}) async-start(s8[9437184]{0:T(1024)(128)(4,1)} %bitcast.89), calls=%async_computation.6 | async-start | bytes 8388608
  704.2 8.8 %slice-start.2 = ((s8[9437184]{0:T(1024)(128)(4,1)}), s8[1048576]{0:T(1024)(128)(4,1)S(1)}, s32[]{:S(2)}) async-start(s8[9437184]{0:T(1024)(128)(4,1)} %bitcast.89), calls=%async_computation.7 | async-start | bytes 2097152
  (11 other events, 23.5 us)
Sparse Core Ops, SparseCore 0:
  379.3 321.2 all-reduce.3
where the time goes:
time: 731 us; the launch traced here: 724 us
  waiting for transfers between devices  239 us (33%)
  local copies, waits for them, and re-layouts  220 us (30%)
  matrix products  117 us (16%)
  blocking collectives  73.8 us (10%)
  other arithmetic  44.7 us (6%)
  between operations  15.3 us (2%)
  starting transfers between devices  13.2 us (2%)
    psum x1, waiting for transfers between devices, shards(): lax.psum((grad_gain_one, grad_shift_one, grad_tok_in, grad_tok_inbias, gr...  155 us
    unnamed x86, local copies, waits for them, and re-layouts  71.9 us
    all_to_all x1, waiting for transfers between devices, shards(): lax.all_to_all(grad_columns, 'mix', split_axis=1, concat_axis=2, tiled=True)  55.4 us
    psum x1, blocking collectives, shards(): lax.psum((grad_gain_one, grad_shift_one, grad_tok_in, grad_tok_inbias, gr...  42.5 us
    all_to_all x1, blocking collectives, shards(): lax.all_to_all(normed, 'mix', split_axis=2, concat_axis=1, tiled=True)  31.3 us
    all_to_all x1, waiting for transfers between devices, shards(): lax.all_to_all(mixed_cols, 'mix', split_axis=1, concat_axis=2, tiled=True)  28.5 us
    convert_element_type x4, local copies, waits for them, and re-layouts, shards(): middle = inputs + mixed.astype(jnp.float32)  27.2 us
    convert_element_type x4, local copies, waits for them, and re-layouts, shards(): grad_normed.astype(jnp.float32)  26.3 us
  transfers between devices with their start and end apart: 4, of which 4 were waited for; matrix products, arithmetic and copies ran while one was open for 13% of the time, Pallas kernels for 0%

commit v1 on v0

--- a/solution.py
+++ b/solution.py
@@ -98,21 +98,24 @@
     grad_inputs, grad_gain_one, grad_shift_one = first_back(grad_normed.astype(jnp.float32))
     patch_grad = (grad_middle + grad_inputs).astype(jnp.bfloat16)
     summed = lax.psum(
-        (
-            grad_gain_one,
-            grad_shift_one,
-            grad_tok_in,
-            grad_tok_inbias,
-            grad_tok_out,
-            grad_tok_outbias,
-            grad_gain_two,
-            grad_shift_two,
-            grad_chan_in,
-            grad_chan_inbias,
-            grad_chan_out,
-            grad_chan_outbias,
+        lax.psum(
+            (
+                grad_gain_one,
+                grad_shift_one,
+                grad_tok_in,
+                grad_tok_inbias,
+                grad_tok_out,
+                grad_tok_outbias,
+                grad_gain_two,
+                grad_shift_two,
+                grad_chan_in,
+                grad_chan_inbias,
+                grad_chan_out,
+                grad_chan_outbias,
+            ),
+            "mix",
         ),
-        ("dp", "mix"),
+        "dp",
     )
     return (
         mixed_out,

time: 731 us -> 1340 us (1.83)
  waiting for transfers between devices: 239 us -> 844 us
    psum x0 -> x1, waiting for transfers between devices: none -> 441 us  [shards(): lax.psum(lax.psum((grad_gain_one, grad_shift_one, grad_tok_in, grad_tok_i...]
    psum x1, waiting for transfers between devices: 155 us -> 336 us  [shards(): lax.psum((grad_gain_one, grad_shift_one, grad_tok_in, grad_tok_inbias, gr...]
    psum x0 -> x1, blocking collectives: none -> 40.5 us  [shards(): lax.psum(lax.psum((grad_gain_one, grad_shift_one, grad_tok_in, grad_tok_i...]
    psum x1, blocking collectives: 42.5 us -> 11.3 us  [shards(): lax.psum((grad_gain_one, grad_shift_one, grad_tok_in, grad_tok_inbias, gr...]
    all_to_all x1, waiting for transfers between devices: 55.4 us -> 37 us  [shards(): lax.all_to_all(grad_columns, 'mix', split_axis=1, concat_axis=2, tiled=True)]
  transfers between devices with their start and end apart: 4 -> 5, of which waited for: 4 -> 5; matrix products, arithmetic and copies ran while one was open for 13% -> 7% of each run, Pallas kernels for 0% -> 0%
where the time goes in v1:
time: 1340 us
  waiting for transfers between devices  844 us (63%)
  local copies, waits for them, and re-layouts  219 us (16%)
  matrix products  117 us (9%)
  blocking collectives  83.2 us (6%)
  other arithmetic  44.8 us (3%)
  between operations  15.4 us (1%)
    psum x1, waiting for transfers between devices, shards(): lax.psum(lax.psum((grad_gain_one, grad_shift_one, grad_tok_in, grad_tok_i...  441 us
    psum x1, waiting for transfers between devices, shards(): lax.psum((grad_gain_one, grad_shift_one, grad_tok_in, grad_tok_inbias, gr...  336 us
    unnamed x86, local copies, waits for them, and re-layouts  70.8 us
    psum x1, blocking collectives, shards(): lax.psum(lax.psum((grad_gain_one, grad_shift_one, grad_tok_in, grad_tok_i...  40.5 us
    all_to_all x1, waiting for transfers between devices, shards(): lax.all_to_all(grad_columns, 'mix', split_axis=1, concat_axis=2, tiled=True)  37 us
    all_to_all x1, blocking collectives, shards(): lax.all_to_all(normed, 'mix', split_axis=2, concat_axis=1, tiled=True)  31.3 us
    all_to_all x1, waiting for transfers between devices, shards(): lax.all_to_all(mixed_cols, 'mix', split_axis=1, concat_axis=2, tiled=True)  28.5 us
    convert_element_type x4, local copies, waits for them, and re-layouts, shards(): middle = inputs + mixed.astype(jnp.float32)  27.2 us
  transfers between devices with their start and end apart: 5, of which 5 were waited for; matrix products, arithmetic and copies ran while one was open for 7% of the time, Pallas kernels for 0%

profile of v1, /device:TPU:0, one launch (start us, length us, event | category | flops | bytes accessed | tf_op | source)
XLA Modules:
  0.0 1336.3 jit_solution(11456076228916010979)
XLA Ops:
  15.3 11.4 copy.67
  26.7 11.5 reshape.138
  38.2 31.3 %all_to_all.54 = bf16[4,2,131712]{2,1,0:T(2,128)(2,1)} all-to-all(bf16[4,2,131712]{2,1,0:T(2,128)(2,1)} %reshape.138), channel_id=1, replica_groups=mesh['dp'=8,'mix'=4] {'mix'}, dimensions={0} | all-to-all | bytes 4214784 | tf_op jit(solution)/shard_map/all_to_all | solution.py:37
  69.6 11.9 reshape.139
  81.5 9.6 copy.68
  96.9 7.8 fusion.17
  109.8 7.4 copy.70
  131.2 28.5 %all-to-all-done.1 = bf16[28,196,192]{2,0,1:T(8,128)(2,1)} async-done(((bf16[28,196,192]{2,0,1:T(8,128)(2,1)}), bf16[28,196,192]{2,0,1:T(8,128)(2,1)}, u32[]{:S(2)}, u32[]{:S(2)}) %all-to-all-start.1) | async-done | bytes 2107424 | tf_op jit(solution)/shard_map/all_to_all | solution.py:47
  159.7 7.5 copy.71
  179.2 7.5 copy.73
  186.7 7.7 reshape.130
  202.5 17.7 %multiply_convert_fusion = (bf16[1372,3072]{1,0:T(8,128)(2,1)}, f32[1372,3072]{1,0:T(8,128)}) fusion(f32[3072]{0:T(1024)S(1)} %copy-done.27, bf16[1372,768]{1,0:T(8,128)(2,1)} %reshape.126, bf16[768,3072]{1,0:T(8,128)(2,1)} %param.25), kind=kOutput, calls=%fused_computation.10 | convolution fusion | flops 6516056064 | bytes 32126976 | tf_op jit(solution)/shard_map/dot_general | solution.py:51
  220.2 19.9 %convert_reduce_fusion = (f32[3072]{0:T(1024)S(1)}, bf16[1372,3072]{1,0:T(8,128)(2,1)S(1)}) fusion(f32[1372,3072]{1,0:T(8,128)} %get-tuple-element.52, f32[3072]{0:T(1024)S(1)} %copy-done.27, bf16[1372,768]{1,0:T(8,128)(2,1)S(1)} %copy-done.11, bf16[3072,768]{1,0:T(8,128)(2,1)} %param.27), kind=kOutput, calls=%fused_computation.9 | convolution fusion | flops 6570845184 | bytes 32139264 | tf_op jit(solution)/shard_map/rc,fc->rf/dot_general | solution.py:66
  240.2 8.3 fusion.41
  258.4 12.2 convolution_add_fusion
  275.8 7.4 fusion.39
  286.0 10.8 copy.74
  296.8 11.5 reshape.140
  312.0 13.2 fusion.43
  325.2 12.2 fusion.42
  337.7 10.9 reshape.141
  348.7 8.6 copy.75
  365.5 9.6 convert_reduce_fusion.1
  379.2 336.4 %all-reduce.9.cloned.1.call-done = (f32[196,384]{1,0:T(8,128)}, f32[384,196]{0,1:T(8,128)}, f32[768,3072]{1,0:T(8,128)}, f32[3072,768]{1,0:T(8,128)}) async-done(((f32[196,384]{1,0:T(8,128)}, f32[384,196]{0,1:T(8,128)}, f32[768,3072]{1,0:T(8,128)}, f32[3072,768]{1,0:T(8,128)}), (f32[196,384]{1,0:T(8,128)}, f32[384,196]{0,1:T(8,128)}, f32[768,3072]{1,0:T(8,128)}, ...) | async-done | bytes 19476496 | tf_op jit(solution)/shard_map/psum | solution.py:101
  720.9 7.5 copy.77
  733.8 37.0 %all-to-all-done.3 = bf16[28,196,192]{2,0,1:T(8,128)(2,1)} async-done(((bf16[28,196,192]{2,0,1:T(8,128)(2,1)}), bf16[28,196,192]{2,0,1:T(8,128)(2,1)}, u32[]{:S(2)}, u32[]{:S(2)}) %all-to-all-start.3) | async-done | bytes 2107424 | tf_op jit(solution)/shard_map/all_to_all | solution.py:97
  788.5 7.6 copy.80
  796.1 7.8 reshape.131
  813.0 11.3 all-reduce.2
  824.3 40.5 %all-reduce = (f32[768]{0:T(1024)}, f32[768]{0:T(1024)}, f32[384]{0:T(512)}, f32[196]{0:T(256)}, f32[768]{0:T(1024)}, /*index=5*/f32[768]{0:T(1024)}, f32[3072]{0:T(1024)}, f32[768]{0:T(1024)}) all-reduce(f32[768]{0:T(1024)S(1)} %get-tuple-element.30, f32[768]{0:T(1024)S(1)} %get-tuple-element.31, ...), channel_id=1, replica_groups=mesh['dp'=8,'mix'=4] {'dp'}, use_global_device_ids=true, to_apply=%region_10.11 | all-reduce | flops 7492 | bytes 59936 | tf_op jit(solution)/shard_map/psum | solution.py:100
  871.6 441.5 %all-reduce.7.cloned.1.call-done = (f32[196,384]{1,0:T(8,128)}, f32[384,196]{0,1:T(8,128)}, f32[768,3072]{1,0:T(8,128)}, f32[3072,768]{1,0:T(8,128)}) async-done(((f32[196,384]{1,0:T(8,128)}, f32[384,196]{0,1:T(8,128)}, f32[768,3072]{1,0:T(8,128)}, f32[3072,768]{1,0:T(8,128)}), (f32[196,384]{1,0:T(8,128)}, f32[384,196]{0,1:T(8,128)}, f32[768,3072]{1,0:T(8,128)}, ...) | async-done | bytes 19476496 | tf_op jit(solution)/shard_map/psum | solution.py:100
  1316.7 8.8 copy.99
  (134 shorter events, 138.0 us)
Async XLA Ops:
  7.2 89.7 %copy-start = (bf16[196,384]{1,0:T(8,128)(2,1)S(1)}, bf16[196,384]{1,0:T(8,128)(2,1)}, u32[]{:S(2)}) copy-start(bf16[196,384]{1,0:T(8,128)(2,1)} %param.19) | copy-start | bytes 451588
  7.2 6.0 copy-start.2
  7.2 6.0 copy-start.19
  7.2 6.0 copy-start.23
  91.1 5.8 copy-start.29
  96.8 9.8 copy-start.25
  96.9 9.8 copy-start.31
  117.1 42.5 %all-to-all-start.1 = ((bf16[28,196,192]{2,0,1:T(8,128)(2,1)}), bf16[28,196,192]{2,0,1:T(8,128)(2,1)}, u32[]{:S(2)}, u32[]{:S(2)}) async-start(bf16[28,196,192]{2,0,1:T(8,128)(2,1)} %copy.70), calls=%async_computation.1 | async-start | bytes 6422528 | tf_op jit(solution)/shard_map/all_to_all | solution.py:47
  202.5 17.7 %copy-start.11 = (bf16[1372,768]{1,0:T(8,128)(2,1)S(1)}, bf16[1372,768]{1,0:T(8,128)(2,1)}, u32[]{:S(2)}) copy-start(bf16[1372,768]{1,0:T(8,128)(2,1)} %reshape.128) | copy-start | bytes 6322180
  202.5 37.7 %slice-start.3 = ((s8[4718592]{0:T(1024)(128)(4,1)}), s8[4194304]{0:T(1024)(128)(4,1)S(1)}, s32[]{:S(2)}) async-start(s8[4718592]{0:T(1024)(128)(4,1)} %bitcast.91), calls=%async_computation.9 | async-start | bytes 8388608
  220.2 20.0 %slice-start.4 = ((s8[4718592]{0:T(1024)(128)(4,1)}), s8[524288]{0:T(1024)(128)(4,1)S(1)}, s32[]{:S(2)}) async-start(s8[4718592]{0:T(1024)(128)(4,1)} %bitcast.91), calls=%async_computation.10 | async-start | bytes 1048576
  240.2 8.4 copy-start.33
  253.7 4.7 copy-start.28
  275.8 9.6 copy-start.6
  308.4 29.4 %all-to-all-start.2 = ((bf16[4,2,131712]{2,1,0:T(2,128)(2,1)}), bf16[4,2,131712]{2,1,0:T(2,128)(2,1)S(1)}, u32[]{:S(2)}, u32[]{:S(2)}) async-start(bf16[4,2,131712]{2,1,0:T(2,128)(2,1)} %reshape.140), calls=%async_computation.2 | async-start | bytes 4214784 | tf_op jit(solution)/shard_map/all_to_all | solution.py:75
  312.0 403.6 %all-reduce.9.cloned.1.call-start = ((), (), s32[]{:S(2)}) async-start(), calls=%async_computation.5 | async-start | bytes 38977536 | tf_op jit(solution)/shard_map/psum | solution.py:101
  312.0 13.2 copy-start.12
  360.2 5.2 copy-start.10
  360.2 5.2 copy-start.26
  360.2 5.3 copy-start.30
  365.4 11.5 copy-start.9
  379.1 934.0 %all-reduce.7.cloned.1.call-start = ((), (), s32[]{:S(2)}) async-start(), calls=%async_computation.4 | async-start | bytes 38977536 | tf_op jit(solution)/shard_map/psum | solution.py:100
  728.4 42.4 %all-to-all-start.3 = ((bf16[28,196,192]{2,0,1:T(8,128)(2,1)}), bf16[28,196,192]{2,0,1:T(8,128)(2,1)}, u32[]{:S(2)}, u32[]{:S(2)}) async-start(bf16[28,196,192]{2,0,1:T(8,128)(2,1)} %copy.77), calls=%async_computation.3 | async-start | bytes 6422528 | tf_op jit(solution)/shard_map/all_to_all | solution.py:97
  777.8 10.8 copy-start.7
  796.1 10.4 copy-start.3
  796.1 10.4 copy-start.14
  796.1 10.4 copy-start.20
  806.2 4.1 copy-start.18
  806.2 4.1 copy-start.16
  1314.8 10.6 slice-start
  1316.7 8.8 slice-start.1
  1316.7 8.8 slice-start.2
  (12 other events, 26.5 us)
Sparse Core Ops, SparseCore 0:
  379.3 336.2 all-reduce.8
  721.2 591.8 all-reduce.6
